TPU v7x, 256 devices: a whole 4x4x8 slice. The times are simulated.
256 devices in a mesh: ctx: 32 (over x, z_hi, y), exp: 8 (over z_lo, core).
Axes of the slice: x: 4, y: 4, z: 8 (z_hi: 2, z_lo: 4; z = z_hi * 4 + z_lo), core: 2. Of those that a mesh axis runs over, the one named last changes fastest.
Arguments:
- queries: bfloat16 [256, 32, 128], P(None, 'exp'), may hold values from -64 to 64
- keys: bfloat16 [32768, 8, 128], P('ctx', 'exp'), may hold values from -8 to 8
- values: bfloat16 [32768, 8, 128], P('ctx', 'exp'), may hold values from -32 to 32
- out_proj: bfloat16 [4096, 4096], P('exp', 'ctx'), may hold values from -0.09375 to 0.09375
- residual: bfloat16 [256, 4096], P('ctx'), may hold values from -6 to 6
- gain: float32 [4096], replicated, may hold values from 0.1 to 1.9
- routes: int32 [256, 2], P('ctx'), may hold values from 0 to 7, all different within a row; in each aligned block of 8 rows (0 to 7, 8 to 15, ...) at most 4 rows name the same one
- gates: float32 [256, 2], P('ctx'), may hold values from 0.25 to 1
- w_gate: bfloat16 [8, 4096, 14336], P('exp', None, 'ctx'), may hold values from -0.09375 to 0.09375
- w_up: bfloat16 [8, 4096, 14336], P('exp', None, 'ctx'), may hold values from -0.09375 to 0.09375
- w_down: bfloat16 [8, 14336, 4096], P('exp', 'ctx'), may hold values from -0.046875 to 0.046875
Outputs:
- mixed: bfloat16 [256, 4096], P('ctx', 'exp')
Inputs may be any that keep to these rules, and one draw needn't show every extreme that they name: `routes`: within each aligned block of 8 rows no expert is named by more than 4 rows, some expert is named by exactly 4 rows in some block, and the 2 experts of a row differ.
All inputs are finite; a program needn't handle non-finite values.
Results may differ from a plain program's by a relative error of at most 0.017.
Values may be sent and summed in bfloat16 or wider, within the bound.
A program may use at most 128 MiB of HBM per device.

v0:
```python
import math
import jax
import jax.numpy as jnp
from jax import lax
from jax.sharding import PartitionSpec as P


def joined(part, axis, combine):
    gathered = jax.tree.map(lambda a: lax.all_gather(a, axis), part)

    def take(source):
        return jax.tree.map(lambda a: lax.dynamic_index_in_dim(a, source, 0, False), gathered)

    return lax.fori_loop(
        1, lax.axis_size(axis), lambda source, state: combine(state, take(source)), take(0)
    )


def combine_parts(first_part, second_part):
    top_level = jnp.maximum(first_part[0], second_part[0])
    first_scale = jnp.exp(first_part[0] - top_level)
    second_scale = jnp.exp(second_part[0] - top_level)
    summed = first_part[1] * first_scale + second_part[1] * second_scale
    weighted = first_part[2] * first_scale[..., None] + second_part[2] * second_scale[..., None]
    return (top_level, summed, weighted)


def local(queries, keys, values, out_proj, residual, gain, routes, gates, w_gate, w_up, w_down):
    tokens_all, heads_local, head_dim = queries.shape
    key_rows, kv_local, unused_dim = keys.shape
    groups = heads_local // kv_local
    ctx_count = lax.axis_size("ctx")
    ctx_index = lax.axis_index("ctx")
    exp_index = lax.axis_index("exp")
    block_rows = residual.shape[0]
    total_len = key_rows * ctx_count
    score_scale = 1.0 / math.sqrt(head_dim)
    grouped = queries.reshape(tokens_all, kv_local, groups, head_dim)
    scores = (
        jnp.einsum("tgrd,sgd->gtrs", grouped, keys, preferred_element_type=jnp.float32)
        * score_scale
    )
    key_pos = ctx_index * key_rows + jnp.arange(key_rows, dtype=jnp.int32)
    query_pos = total_len - tokens_all + jnp.arange(tokens_all, dtype=jnp.int32)
    visible = (key_pos[None, :] <= query_pos[:, None])[None, :, None, :]
    scores = jnp.where(visible, scores, jnp.float32(-1e30))
    block_max = jnp.max(scores, axis=-1)
    expw = jnp.where(visible, jnp.exp(scores - block_max[..., None]), jnp.float32(0.0))
    block_sum = jnp.sum(expw, axis=-1)
    block_out = jnp.einsum(
        "gtrs,sgd->gtrd", expw.astype(jnp.bfloat16), values, preferred_element_type=jnp.float32
    )
    merged = joined((block_max, block_sum, block_out), "ctx", combine_parts)
    attended_all = merged[2] / merged[1][..., None]
    own_rows = lax.dynamic_slice_in_dim(attended_all, ctx_index * block_rows, block_rows, 1)
    attended = (
        own_rows.transpose(1, 0, 2, 3)
        .reshape(block_rows, heads_local * head_dim)
        .astype(jnp.bfloat16)
    )
    partial_value = jnp.dot(
        attended,
        lax.all_gather(out_proj, "ctx", axis=1, tiled=True),
        preferred_element_type=jnp.float32,
    )
    stream = residual.astype(jnp.float32) + lax.psum(
        partial_value.astype(jnp.bfloat16), "exp"
    ).astype(jnp.float32)
    normed = (
        stream * lax.rsqrt(jnp.mean(stream * stream, axis=-1, keepdims=True) + 1e-05) * gain
    ).astype(jnp.bfloat16)
    experts_local = w_gate.shape[0]
    expert_count = experts_local * lax.axis_size("exp")
    top_count = routes.shape[1]
    capacity = min(block_rows, 2 * top_count * block_rows // expert_count)
    flat_ids = routes.reshape(block_rows * top_count)
    onehot = (flat_ids[:, None] == jnp.arange(expert_count, dtype=jnp.int32)[None, :]).astype(
        jnp.int32
    )
    before = jnp.cumsum(onehot, axis=0, dtype=jnp.int32) - onehot
    slot_of = jnp.sum(before * onehot, axis=1, dtype=jnp.int32)
    mine_ids = exp_index * experts_local + jnp.arange(experts_local, dtype=jnp.int32)
    is_mine = flat_ids[:, None] == mine_ids[None, :]
    slot_hit = is_mine[:, :, None] & (
        slot_of[:, None, None] == jnp.arange(capacity, dtype=jnp.int32)[None, None, :]
    )
    slot_hit = slot_hit.astype(jnp.float32).reshape(block_rows, top_count, experts_local, capacity)
    dispatch_map = jnp.sum(slot_hit, axis=1)
    combine_map = jnp.sum(slot_hit * gates[:, :, None, None], axis=1)
    buffer = jnp.einsum(
        "tec,td->ced", dispatch_map.astype(jnp.bfloat16), normed, preferred_element_type=jnp.float32
    ).astype(jnp.bfloat16)
    shard_rows = lax.all_gather(buffer, "ctx", axis=0, tiled=True)
    gate_val = jnp.einsum("ned,edf->nef", shard_rows, w_gate, preferred_element_type=jnp.float32)
    up_val = jnp.einsum("ned,edf->nef", shard_rows, w_up, preferred_element_type=jnp.float32)
    act = (jax.nn.silu(gate_val) * up_val).astype(jnp.bfloat16)
    expert_out = lax.psum_scatter(
        jnp.einsum("nef,efd->ned", act, w_down, preferred_element_type=jnp.float32).astype(
            jnp.bfloat16
        ),
        "ctx",
        scatter_dimension=0,
        tiled=True,
    ).astype(jnp.float32)
    contribution = jnp.einsum(
        "tec,ced->td", combine_map, expert_out, precision=lax.Precision.HIGHEST
    )
    moe_share = lax.psum_scatter(
        contribution.astype(jnp.bfloat16), "exp", scatter_dimension=1, tiled=True
    ).astype(jnp.float32)
    feat_width = moe_share.shape[1]
    own_stream = lax.dynamic_slice_in_dim(stream, exp_index * feat_width, feat_width, 1)
    return (own_stream + moe_share).astype(jnp.bfloat16)


def solution(mesh):
    return jax.shard_map(
        local,
        mesh=mesh,
        in_specs=(
            P(None, "exp", None),
            P("ctx", "exp", None),
            P("ctx", "exp", None),
            P("exp", "ctx"),
            P("ctx", None),
            P(),
            P("ctx", None),
            P("ctx", None),
            P("exp", None, "ctx"),
            P("exp", None, "ctx"),
            P("exp", "ctx", None),
        ),
        out_specs=P("ctx", "exp"),
        check_vma=False,
    )
```

profile of v0, /device:TPU:2, one launch (start us, length us, event | category | flops | bytes accessed | tf_op | source)
XLA Modules:
  0.0 1042.4 jit_solution(11815722336202214809)
XLA Ops:
  7.5 2.0 fusion.8
  9.5 2.0 copy-done.1
  11.4 2.2 fusion.16
  14.5 3.7 fusion.15
  18.1 112.5 %all-gather = f32[8192,4]{0,1:T(4,128)S(1)} all-gather(f32[256,4]{0,1:T(4,128)S(1)} %get-tuple-element.241), channel_id=2, replica_groups=mesh['ctx'=32,'exp'=8] {'ctx'}, dimensions={0}, use_global_device_ids=true | all-gather | bytes 135168 | tf_op jit(solution)/shard_map/all_gather | solution.py:9
  130.7 123.6 %all-gather.1 = f32[8192,4]{0,1:T(4,128)S(1)} all-gather(f32[256,4]{0,1:T(4,128)S(1)} %fusion.15), channel_id=3, replica_groups=mesh['ctx'=32,'exp'=8] {'ctx'}, dimensions={0}, use_global_device_ids=true | all-gather | bytes 135168 | tf_op jit(solution)/shard_map/all_gather | solution.py:9
  254.9 12.9 %all-gather.11.cloned.1.call-done = f32[8192,4,128]{2,0,1:T(8,128)} async-done(((f32[256,4,128]{2,0,1:T(8,128)}), f32[8192,4,128]{2,0,1:T(8,128)}) %all-gather.11.cloned.1.call-update) | async-done | bytes 16777232 | tf_op jit(solution)/shard_map/all_gather | solution.py:9
  269.3 84.7 %while.19 = (s32[]{:T(128)}, f32[1,256,4]{1,2,0:T(4,128)S(1)}, f32[1,256,4]{1,2,0:T(4,128)S(1)}, f32[1,256,4,128]{3,2,1,0:T(4,128)S(1)}, f32[32,1,256,4]{2,3,1,0...) while((s32[]{:T(128)}, f32[1,256,4]{1,2,0:T(4,128)S(1)}, ...), condition=%wide.region_3.4_spmd, body=%wide.region_2.3_spmd.sunk | while | flops 400389 | bytes 2699419 | solution.py:14
  270.8 1.3 fusion.75
  273.5 1.3 fusion.75
  279.0 1.3 fusion.75
  287.2 1.3 fusion.75
  292.6 1.3 fusion.75
  300.8 1.3 fusion.75
  309.0 1.3 fusion.75
  317.2 1.3 fusion.75
  325.4 1.3 fusion.75
  330.9 1.3 fusion.75
  333.6 1.3 fusion.75
  336.4 1.3 fusion.75
  344.5 1.3 fusion.75
  350.0 1.3 fusion.75
  354.3 45.0 %all-gather.7.cloned.1.call-done = bf16[512,4096]{1,0:T(8,128)(2,1)} async-done(((bf16[512,128]{1,0:T(8,128)(2,1)}), bf16[512,4096]{1,0:T(8,128)(2,1)}) %all-gather.7.cloned.1.call-update) | async-done | bytes 4194320 | tf_op jit(solution)/shard_map/all_gather | solution.py:63
  399.3 3.5 convolution_convert_fusion.2
  402.9 65.4 %all-reduce.4.cloned.1.call-done = bf16[8,4096]{1,0:T(8,128)(2,1)} async-done(((bf16[8,4096]{1,0:T(8,128)(2,1)}), bf16[8,4096]{1,0:T(8,128)(2,1)}) %all-reduce.4.cloned.1.call-update) | async-done | bytes 65552 | tf_op jit(solution)/shard_map/psum | solution.py:66
  471.1 90.5 %all-gather.9.cloned.1.call-done = bf16[128,1,4096]{2,1,0:T(2,128)(2,1)} async-done(((bf16[4,1,4096]{2,1,0:T(2,128)(2,1)}), bf16[128,1,4096]{2,1,0:T(2,128)(2,1)}) %all-gather.9.cloned.1.call-update) | async-done | bytes 1048592 | tf_op jit(solution)/shard_map/all_gather | solution.py:93
  561.6 4.8 fusion.19
  566.4 7.3 fusion.6
  574.9 405.6 %all-reduce.6.cloned.1.call-done = bf16[128,1,4096]{2,0,1:T(8,128)(2,1)} async-done(((bf16[128,1,4096]{2,0,1:T(8,128)(2,1)}), bf16[128,1,4096]{2,0,1:T(8,128)(2,1)}) %all-reduce.6.cloned.1.call-update) | async-done | bytes 1048592
  980.5 1.7 convolution_convert_fusion.1
  982.3 52.0 %reduce-scatter.3.cloned.1.call-done = bf16[8,512]{1,0:T(8,128)(2,1)} async-done(((bf16[8,4096]{1,0:T(8,128)(2,1)}), bf16[8,512]{1,0:T(8,128)(2,1)}) %reduce-scatter.3.cloned.1.call-update) | async-done | bytes 8208 | tf_op jit(solution)/shard_map/reduce_scatter | solution.py:108
  1034.3 1.3 add_convert_fusion
  (256 shorter events, 72.5 us)
Async XLA Ops:
  6.5 1.0 copy-start
  6.5 4.9 copy-start.7
  6.5 261.3 %all-gather.11.cloned.1.call-start = ((), (), s32[]{:S(2)}) async-start(), calls=%async_computation.5 | async-start | bytes 17301504 | tf_op jit(solution)/shard_map/all_gather | solution.py:9
  9.4 2.0 copy-start.1
  13.6 240.7 %copy-start.5 = (s32[8,2]{0,1:T(2,128)S(1)}, s32[8,2]{0,1:T(2,128)}, u32[]{:S(2)}) copy-start(s32[8,2]{0,1:T(2,128)} %param.19) | copy-start | bytes 196
  13.7 385.6 %all-gather.7.cloned.1.call-start = ((), (), s32[]{:S(2)}) async-start(), calls=%async_computation.1 | async-start | bytes 4325376 | tf_op jit(solution)/shard_map/all_gather | solution.py:63
  14.4 453.8 %all-reduce.4.cloned.1.call-start = ((), (), s32[]{:S(2)}) async-start(), calls=%async_computation.2 | async-start | bytes 131072 | tf_op jit(solution)/shard_map/psum | solution.py:66
  354.0 48.8 %copy-start.6 = (f32[8,2]{0,1:T(2,128)S(1)}, f32[8,2]{0,1:T(2,128)}, u32[]{:S(2)}) copy-start(f32[8,2]{0,1:T(2,128)} %param.20) | copy-start | bytes 196
  354.0 114.2 %copy-start.3 = (bf16[8,4096]{1,0:T(8,128)(2,1)S(1)}, bf16[8,4096]{1,0:T(8,128)(2,1)}, u32[]{:S(2)}) copy-start(bf16[8,4096]{1,0:T(8,128)(2,1)} %param.17) | copy-start | bytes 196612
  354.1 115.2 %copy-start.4 = (f32[4096]{0:T(1024)S(1)}, f32[4096]{0:T(1024)}, u32[]{:S(2)}) copy-start(f32[4096]{0:T(1024)} %param.18) | copy-start | bytes 49156
  402.8 158.8 %all-gather.9.cloned.1.call-start = ((), (), s32[]{:S(2)}) async-start(), calls=%async_computation.3 | async-start | bytes 2162688 | tf_op jit(solution)/shard_map/all_gather | solution.py:93
  471.0 509.5 %all-reduce.6.cloned.1.call-start = ((), (), s32[]{:S(2)}) async-start(), calls=%async_computation.6 | async-start | bytes 2097152
  561.6 4.8 copy-start.2
  566.3 7.4 copy-start.8
  573.6 460.6 %reduce-scatter.3.cloned.1.call-start = ((), (), s32[]{:S(2)}) async-start(), calls=%async_computation.4 | async-start | bytes 73728 | tf_op jit(solution)/shard_map/reduce_scatter | solution.py:108
Sparse Core Ops, SparseCore 0:
  13.8 254.0 all-gather.10
  271.1 128.1 all-gather.6
  402.9 65.3 all-reduce.3
  472.2 89.3 all-gather.8
  573.8 406.6 all-reduce.5
  982.9 51.3 reduce-scatter.2
where the time goes:
time: 1040 us
  waiting for transfers between devices  672 us (65%)
  blocking collectives  236 us (23%)
  local copies, waits for them, and re-layouts  48.1 us (5%)
  other arithmetic  47.1 us (5%)
  matrix products  22.4 us (2%)
  between operations  14.3 us (1%)
    unnamed x7, waiting for transfers between devices  406 us
    all_gather x2, blocking collectives, joined(): gathered = jax.tree.map(lambda a: lax.all_gather(a, axis), part)  236 us
    all_gather x1, waiting for transfers between devices, local(): shard_rows = lax.all_gather(buffer, 'ctx', axis=0, tiled=True)  90.5 us
    psum x1, waiting for transfers between devices, local(): lax.psum(partial_value.astype(jnp.bfloat16), 'exp').astype(jnp.float32)  65.4 us
    reduce_scatter x1, waiting for transfers between devices, local(): lax.psum_scatter(contribution.astype(jnp.bfloat16), 'exp', scatter_dimens...  52 us
    all_gather x1, waiting for transfers between devices, local(): lax.all_gather(out_proj, 'ctx', axis=1, tiled=True)  45 us
    add x31, other arithmetic, combine_parts(): first_part[2] * first_scale[..., None]  39.3 us
    dynamic_slice x31, local copies, waits for them, and re-layouts, take(): lax.dynamic_index_in_dim(a, source, 0, False)  33.8 us
  transfers between devices with their start and end apart: 6, of which 6 were waited for; matrix products, arithmetic and copies ran while one was open for 9% of the time, Pallas kernels for 0%

commit v1 on v0

--- a/solution.py
+++ b/solution.py
@@ -63,8 +63,12 @@
         lax.all_gather(out_proj, "ctx", axis=1, tiled=True),
         preferred_element_type=jnp.float32,
     )
-    stream = residual.astype(jnp.float32) + lax.psum(
-        partial_value.astype(jnp.bfloat16), "exp"
+
+    def try_all_series(point, across="exp"):
+        return jnp.sum(jax.lax.all_gather(point, across), axis=0)
+
+    stream = residual.astype(jnp.float32) + try_all_series(
+        partial_value.astype(jnp.bfloat16)
     ).astype(jnp.float32)
     normed = (
         stream * lax.rsqrt(jnp.mean(stream * stream, axis=-1, keepdims=True) + 1e-05) * gain

time: 1040 us -> 988 us (0.950)
  waiting for transfers between devices: 672 us -> 603 us
  blocking collectives: 236 us -> 251 us
    psum x1 -> x0, waiting for transfers between devices: 65.4 us -> none  [local(): lax.psum(partial_value.astype(jnp.bfloat16), 'exp').astype(jnp.float32)]
    all_gather x0 -> x1, blocking collectives: none -> 14.9 us  [try_all_series(): return jnp.sum(jax.lax.all_gather(point, across), axis=0)]
    unnamed x7 -> x6, waiting for transfers between devices: 406 us -> 406 us
  transfers between devices with their start and end apart: 6 -> 5, of which waited for: 6 -> 5; matrix products, arithmetic and copies ran while one was open for 9% -> 9% of each run, Pallas kernels for 0% -> 0%
where the time goes in v1:
time: 988 us; the launch traced here: 986 us
  waiting for transfers between devices  603 us (61%)
  blocking collectives  251 us (25%)
  local copies, waits for them, and re-layouts  48.1 us (5%)
  other arithmetic  46.3 us (5%)
  matrix products  21 us (2%)
  between operations  14 us (1%)
    unnamed x6, waiting for transfers between devices  406 us
    all_gather x2, blocking collectives, joined(): gathered = jax.tree.map(lambda a: lax.all_gather(a, axis), part)  236 us
    all_gather x1, waiting for transfers between devices, local(): shard_rows = lax.all_gather(buffer, 'ctx', axis=0, tiled=True)  86.5 us
    reduce_scatter x1, waiting for transfers between devices, local(): lax.psum_scatter(contribution.astype(jnp.bfloat16), 'exp', scatter_dimens...  52.2 us
    all_gather x1, waiting for transfers between devices, local(): lax.all_gather(out_proj, 'ctx', axis=1, tiled=True)  45 us
    add x31, other arithmetic, combine_parts(): first_part[2] * first_scale[..., None]  39.3 us
    dynamic_slice x31, local copies, waits for them, and re-layouts, take(): lax.dynamic_index_in_dim(a, source, 0, False)  33.8 us
  transfers between devices with their start and end apart: 5, of which 5 were waited for; matrix products, arithmetic and copies ran while one was open for 9% of the time, Pallas kernels for 0%

profile of v1, /device:TPU:2, one launch (start us, length us, event | category | flops | bytes accessed | tf_op | source)
XLA Modules:
  0.0 985.8 jit_solution(14726933974939099324)
XLA Ops:
  7.5 2.0 fusion.8
  9.5 2.0 copy-done.1
  11.4 2.2 fusion.16
  14.5 3.7 fusion.15
  18.1 112.6 %all-gather = f32[8192,4]{0,1:T(4,128)S(1)} all-gather(f32[256,4]{0,1:T(4,128)S(1)} %get-tuple-element.241), channel_id=2, replica_groups=mesh['ctx'=32,'exp'=8] {'ctx'}, dimensions={0}, use_global_device_ids=true | all-gather | bytes 135168 | tf_op jit(solution)/shard_map/all_gather | solution.py:9
  130.7 123.6 %all-gather.1 = f32[8192,4]{0,1:T(4,128)S(1)} all-gather(f32[256,4]{0,1:T(4,128)S(1)} %fusion.15), channel_id=3, replica_groups=mesh['ctx'=32,'exp'=8] {'ctx'}, dimensions={0}, use_global_device_ids=true | all-gather | bytes 135168 | tf_op jit(solution)/shard_map/all_gather | solution.py:9
  254.9 13.0 %all-gather.12.cloned.1.call-done = f32[8192,4,128]{2,0,1:T(8,128)} async-done(((f32[256,4,128]{2,0,1:T(8,128)}), f32[8192,4,128]{2,0,1:T(8,128)}) %all-gather.12.cloned.1.call-update) | async-done | bytes 16777232 | tf_op jit(solution)/shard_map/all_gather | solution.py:9
  269.3 84.7 %while.19 = (s32[]{:T(128)}, f32[1,256,4]{1,2,0:T(4,128)S(1)}, f32[1,256,4]{1,2,0:T(4,128)S(1)}, f32[1,256,4,128]{3,2,1,0:T(4,128)S(1)}, f32[32,1,256,4]{2,3,1,0...) while((s32[]{:T(128)}, f32[1,256,4]{1,2,0:T(4,128)S(1)}, ...), condition=%wide.region_3.4_spmd, body=%wide.region_2.3_spmd.sunk | while | flops 400389 | bytes 2699419 | solution.py:14
  270.8 1.3 fusion.75
  273.5 1.3 fusion.75
  281.7 1.3 fusion.75
  284.4 1.3 fusion.75
  289.9 1.3 fusion.75
  298.1 1.3 fusion.75
  306.3 1.3 fusion.75
  314.5 1.3 fusion.75
  319.9 1.3 fusion.75
  322.7 1.3 fusion.75
  328.1 1.3 fusion.75
  339.1 1.3 fusion.75
  341.8 1.3 fusion.75
  347.3 1.3 fusion.75
  354.3 45.0 %all-gather.8.cloned.1.call-done = bf16[512,4096]{1,0:T(8,128)(2,1)} async-done(((bf16[512,128]{1,0:T(8,128)(2,1)}), bf16[512,4096]{1,0:T(8,128)(2,1)}) %all-gather.8.cloned.1.call-update) | async-done | bytes 4194320 | tf_op jit(solution)/shard_map/all_gather | solution.py:63
  399.3 2.8 convolution_convert_fusion.2
  402.1 14.9 %all-gather.3 = bf16[64,4096]{1,0:T(8,128)(2,1)S(1)} all-gather(bf16[8,4096]{1,0:T(8,128)(2,1)S(1)} %convolution_convert_fusion.2), channel_id=5, replica_groups=mesh['ctx'=32,'exp'=8] {'exp'}, dimensions={0}, use_global_device_ids=true | all-gather | bytes 589824 | tf_op jit(solution)/shard_map/all_gather | solution.py:68
  418.5 86.5 %all-gather.10.cloned.1.call-done = bf16[128,1,4096]{2,1,0:T(2,128)(2,1)} async-done(((bf16[4,1,4096]{2,1,0:T(2,128)(2,1)}), bf16[128,1,4096]{2,1,0:T(2,128)(2,1)}) %all-gather.10.cloned.1.call-update) | async-done | bytes 1048592 | tf_op jit(solution)/shard_map/all_gather | solution.py:97
  505.0 4.8 fusion.19
  509.8 7.3 fusion.6
  518.4 405.6 %all-reduce.3.cloned.1.call-done = bf16[128,1,4096]{2,0,1:T(8,128)(2,1)} async-done(((bf16[128,1,4096]{2,0,1:T(8,128)(2,1)}), bf16[128,1,4096]{2,0,1:T(8,128)(2,1)}) %all-reduce.3.cloned.1.call-update) | async-done | bytes 1048592
  924.1 1.7 convolution_convert_fusion.1
  925.8 52.2 %reduce-scatter.3.cloned.1.call-done = bf16[8,512]{1,0:T(8,128)(2,1)} async-done(((bf16[8,4096]{1,0:T(8,128)(2,1)}), bf16[8,512]{1,0:T(8,128)(2,1)}) %reduce-scatter.3.cloned.1.call-update) | async-done | bytes 8208 | tf_op jit(solution)/shard_map/reduce_scatter | solution.py:112
  978.0 1.3 add_convert_fusion
  (255 shorter events, 71.1 us)
Async XLA Ops:
  6.5 1.0 copy-start
  6.5 4.9 copy-start.7
  6.5 261.4 %all-gather.12.cloned.1.call-start = ((), (), s32[]{:S(2)}) async-start(), calls=%async_computation.4 | async-start | bytes 17301504 | tf_op jit(solution)/shard_map/all_gather | solution.py:9
  9.4 2.0 copy-start.1
  13.6 240.6 %copy-start.5 = (s32[8,2]{0,1:T(2,128)S(1)}, s32[8,2]{0,1:T(2,128)}, u32[]{:S(2)}) copy-start(s32[8,2]{0,1:T(2,128)} %param.19) | copy-start | bytes 196
  13.6 241.2 %copy-start.6 = (f32[8,2]{0,1:T(2,128)S(1)}, f32[8,2]{0,1:T(2,128)}, u32[]{:S(2)}) copy-start(f32[8,2]{0,1:T(2,128)} %param.20) | copy-start | bytes 196
  13.7 385.6 %all-gather.8.cloned.1.call-start = ((), (), s32[]{:S(2)}) async-start(), calls=%async_computation.1 | async-start | bytes 4325376 | tf_op jit(solution)/shard_map/all_gather | solution.py:63
  14.4 490.6 %all-gather.10.cloned.1.call-start = ((), (), s32[]{:S(2)}) async-start(), calls=%async_computation.2 | async-start | bytes 2162688 | tf_op jit(solution)/shard_map/all_gather | solution.py:97
  354.0 63.1 %copy-start.3 = (bf16[8,4096]{1,0:T(8,128)(2,1)S(1)}, bf16[8,4096]{1,0:T(8,128)(2,1)}, u32[]{:S(2)}) copy-start(bf16[8,4096]{1,0:T(8,128)(2,1)} %param.17) | copy-start | bytes 196612
  354.1 63.3 %copy-start.4 = (f32[4096]{0:T(1024)S(1)}, f32[4096]{0:T(1024)}, u32[]{:S(2)}) copy-start(f32[4096]{0:T(1024)} %param.18) | copy-start | bytes 49156
  418.2 505.8 %all-reduce.3.cloned.1.call-start = ((), (), s32[]{:S(2)}) async-start(), calls=%async_computation.5 | async-start | bytes 2097152
  505.0 4.8 copy-start.2
  509.8 7.4 copy-start.8
  517.1 460.9 %reduce-scatter.3.cloned.1.call-start = ((), (), s32[]{:S(2)}) async-start(), calls=%async_computation.3 | async-start | bytes 73728 | tf_op jit(solution)/shard_map/reduce_scatter | solution.py:112
Sparse Core Ops, SparseCore 0:
  13.8 254.0 all-gather.11
  271.1 128.1 all-gather.7
  418.4 86.5 all-gather.9
  517.3 406.7 all-reduce.2
  926.6 51.3 reduce-scatter.2
